TPU v7x, 256 devices: a whole 4x4x8 slice. The times are simulated.
256 devices in a mesh: leaf: 256 (over z, y, x, core).
Axes of the slice: x: 4, y: 4, z: 8, core: 2. Of those that a mesh axis runs over, the one named last changes fastest.
Arguments:
- samples: float32 [131072, 1024], P('leaf'), may hold values from -6 to 6
- test_vectors: float32 [131072, 1024], P('leaf'), may hold values from -6 to 6
- diag_blocks: float32 [131072, 512], P('leaf'), may hold values from -0.25 to 0.25
- leaf_skeleton: int32 [256, 128], P('leaf'), may hold values from 0 to 511, as said below
- leaf_rank: int32 [256], replicated, may hold values from 64 to 128, as said below
- coupling_1: float32 [32768, 128], P('leaf'), may hold values from -0.5 to 0.5
- coupling_2: float32 [16384, 128], P('leaf'), may hold values from -0.5 to 0.5
- coupling_3: float32 [8192, 128], P('leaf'), may hold values from -0.5 to 0.5
- skeleton_1: int32 [128, 128], replicated, may hold values from 0 to 255, as said below
- rank_1: int32 [128], replicated, may hold values from 64 to 128, as said below
- skeleton_2: int32 [64, 128], replicated, may hold values from 0 to 255, as said below
- rank_2: int32 [64], replicated, may hold values from 64 to 128, as said below
- skeleton_3: int32 [32, 128], replicated, may hold values from 0 to 255, as said below
- rank_3: int32 [32], replicated, may hold values from 64 to 128, as said below
Outputs:
- leaf_basis: float32 [131072, 128], P('leaf')
- basis_1: float32 [32768, 128], P('leaf')
- basis_2: float32 [16384, 128], P('leaf')
- basis_3: float32 [8192, 128], P('leaf')
- top_samples: float32 [4096, 1024], P('leaf')
- top_projected: float32 [4096, 1024], P('leaf')
Inputs may be any that keep to these rules, and one draw needn't show every extreme that they name: `leaf_skeleton`: each row lists 128 different ports of its leaf. Only the first leaf_rank[n] entries of skeleton row n count; some leaf has rank 128 and some 128 // 2. `skeleton_1`: row n lists 128 different rows of node n's stacked samples (rows below 128 from the first child, the rest from the second); its first rank_1[n] entries are live rows, below the child's rank within its half. `rank_1`: some node has rank 128 and some 128 // 2. `skeleton_2`: as skeleton_1, for level 2 nodes. `rank_2`: some node has rank 128 and some 128 // 2. `skeleton_3`: as skeleton_1, for level 3 nodes. `rank_3`: some node has rank 128 and some 128 // 2.
All inputs are finite; a program needn't handle non-finite values.
Results may differ from a plain program's by a relative error of at most 0.0003.
Values sent between devices are 32-bit elements; how exact they have to be, the bound alone decides.
A program may use at most 64 MiB of HBM per device.

v0:
```python
import jax
import jax.numpy as jnp
from jax import lax
from jax.experimental import pallas as pl
from jax.experimental.pallas import tpu as pltpu
from jax.sharding import PartitionSpec as P

RING = 8
K = 128
LEAF = 512
SAMPLES = 1024
CHUNK = 256
STEPS = SAMPLES // CHUNK
F32 = jnp.float32
BF16 = jnp.bfloat16
NN = (((1,), (0,)), ((), ()))
NT = (((1,), (1,)), ((), ()))


def dot(left, right, dims=NN):
    return lax.dot_general(left, right, dims, preferred_element_type=F32)


def split(value):
    high = value.astype(BF16)
    low = (value - high.astype(F32)).astype(BF16)
    return high, low


def dot3(left, right, dims=NN):
    small = dot(left[0], right[1], dims) + dot(left[1], right[0], dims)
    return dot(left[0], right[0], dims) + small


def spread_ratios(count):
    ratios = [2.0 * K + 1.0]
    for _ in range(count):
        last = ratios[-1]
        ratios.append((last + 1.0) ** 2 / (4.0 * last))
    return ratios


def inverse(gram, rank):
    row = lax.broadcasted_iota(jnp.int32, (K, K), 0)
    col = lax.broadcasted_iota(jnp.int32, (K, K), 1)
    eye = jnp.where(row == col, 1.0, 0.0).astype(F32)
    total = jnp.sum(jnp.sum(gram * eye, axis=0, keepdims=True), axis=1, keepdims=True)
    ridge = 0.5 * total / rank + 1e-06
    shrink = 1.0 / ridge
    system = gram * shrink + eye
    ratios = spread_ratios(6)
    parts = split(system)
    first = ratios[0]
    approx = ((first + 1.0) * eye - system) * (1.0 / first)
    product = ((first + 1.0) * system - dot3(parts, parts)) * (1.0 / first)
    for step in range(1, 6):
        ratio = ratios[step]
        factor = split(((ratio + 1.0) * eye - product) * (1.0 / ratio))
        approx = dot3(split(approx), factor)
        if step < 5:
            product = dot3(split(product), factor)
    approx = approx * (2.0 / (1.0 + ratios[6]))
    residual = eye - lax.dot_general(
        system, approx, NN, precision=lax.Precision.HIGHEST, preferred_element_type=F32
    )
    approx = approx + dot3(split(approx), split(residual))
    return approx * shrink


def selector(skeleton_row, rank, width):
    wide = jnp.transpose(jnp.broadcast_to(skeleton_row, (K, K)))
    live = lax.broadcasted_iota(jnp.int32, (K, K), 0) < rank
    blocks = []
    for block in range(width // K):
        want = lax.broadcasted_iota(jnp.int32, (K, K), 1) + block * K
        blocks.append(jnp.where((wide == want) & live, 1.0, 0.0).astype(BF16))
    return jnp.concatenate(blocks, axis=1)


def body(
    stride,
    samples,
    tests,
    diag,
    leaf_skeleton,
    skeleton_1,
    skeleton_2,
    skeleton_3,
    coupling_1,
    coupling_2,
    coupling_3,
    leaf_rank,
    rank_1,
    rank_2,
    rank_3,
    leaf_basis,
    basis_1,
    basis_2,
    basis_3,
    top_samples,
    top_projected,
    s_buf,
    w_buf,
    d_buf,
    d_high,
    d_low,
    w_high,
    w_low,
    out_c,
    out_p,
    c_1,
    p_1,
    c_2,
    p_2,
    c_3,
    p_3,
    c_top,
    p_top,
    e_1,
    e_2,
    e_3,
    kept_high,
    kept_low,
    basis_leaf,
    basis_buf_1,
    basis_buf_2,
    basis_buf_3,
    load_sem,
    leaf_out_sem,
    e_send,
    e_recv_1,
    e_recv_2,
    e_recv_3,
    c_send,
    p_send,
    c_recv_1,
    p_recv_1,
    c_recv_2,
    p_recv_2,
    c_recv_3,
    p_recv_3,
    out_send_1,
    out_send_2,
    out_send_3,
    top_send_c,
    top_send_p,
    out_recv,
):
    device = lax.axis_index("leaf")
    rest = device % stride
    z = device // stride
    shift = (rest % 2) * (RING // 2)
    pos = (z + RING - shift) % RING

    def at_z(where):
        return where * stride + rest

    def at_pos(where):
        return at_z((where + shift) % RING)

    def remote(src, dst, send, recv, target):
        return pltpu.make_async_remote_copy(
            src_ref=src,
            dst_ref=dst,
            send_sem=send,
            recv_sem=recv,
            device_id=(target,),
            device_id_type=pl.DeviceIdType.MESH,
        )

    def push(src, dst, send, recv, target):
        @pl.when(target != device)
        def _():
            remote(src, dst, send, recv, target).start()

        @pl.when(target == device)
        def _():
            pltpu.make_async_copy(src, dst, recv).start()

    def pushed(src, dst, send, recv, target):
        @pl.when(target != device)
        def _():
            remote(src, dst, send, recv, target).wait_send()

    def arrived(dst, recv):
        pltpu.make_async_copy(dst, dst, recv).wait()

    load_d = pltpu.make_async_copy(diag, d_buf, load_sem.at[0])
    load_d.start()
    loads_w, loads_s = [], []
    for k in range(STEPS):
        span = pl.ds(k * CHUNK, CHUNK)
        loads_w.append(pltpu.make_async_copy(tests.at[:, span], w_buf.at[k], load_sem.at[1 + 2 * k]))
        loads_s.append(pltpu.make_async_copy(samples.at[:, span], s_buf.at[k], load_sem.at[2 + 2 * k]))
        loads_w[k].start()
        loads_s[k].start()

    barrier = pltpu.get_barrier_semaphore()
    for hop in range(1, RING):
        pl.semaphore_signal(
            barrier,
            inc=1,
            device_id=(at_z((z + hop) % RING),),
            device_id_type=pl.DeviceIdType.MESH,
        )

    node_leaf = z % 4
    child_leaf = z // 4
    home_1 = at_pos(node_leaf // 2 + 2 * (1 - node_leaf % 2))
    node_1 = 2 * (pos % 2) + 1 - (pos % 4) // 2
    node_2 = node_1 % 2
    child_1 = pos % 2
    home_2 = at_pos(2 - node_2)
    child_2 = node_2
    home_3 = at_pos(1)

    select = selector(leaf_skeleton[...], leaf_rank[device], LEAF)
    load_d.wait()
    for r in range(4):
        rows = pl.ds(r * K, K)
        high, low = split(d_buf[rows, :])
        d_high[rows, :] = high
        d_low[rows, :] = low

    home_e2 = at_pos(2 - z % 2)
    c2, h2 = (z // 2) % 2, z // 4
    c3, h3 = z % 2, z // 2
    moves_e = (
        (coupling_1, e_1.at[child_leaf], e_send.at[0], e_recv_1.at[child_leaf], home_1),
        (
            coupling_2,
            e_2.at[c2, pl.ds(pl.multiple_of(h2 * 64, 64), 64)],
            e_send.at[1],
            e_recv_2.at[c2, h2],
            home_e2,
        ),
        (
            coupling_3,
            e_3.at[c3, pl.ds(pl.multiple_of(h3 * 32, 32), 32)],
            e_send.at[2],
            e_recv_3.at[c3, h3],
            home_3,
        ),
    )

    cross = [jnp.zeros((K, K), F32) for _ in range(4)]
    gram = jnp.zeros((K, K), F32)
    moves_c, moves_p = [], []
    for k in range(STEPS):
        loads_w[k].wait()
        loads_s[k].wait()
        high, low = split(w_buf[k])
        w_high[k] = high
        w_low[k] = low
        w_parts = (w_high[k], w_low[k])
        parts = []
        chosen_high = jnp.zeros((K, CHUNK), F32)
        chosen_low = jnp.zeros((K, CHUNK), F32)
        for r in range(4):
            rows = pl.ds(r * K, K)
            local = s_buf[k, rows, :] - dot3((d_high[rows, :], d_low[rows, :]), w_parts)
            part = split(local)
            parts.append(part)
            columns = select[:, r * K : (r + 1) * K]
            chosen_high = chosen_high + dot(columns, part[0])
            chosen_low = chosen_low + dot(columns, part[1])
        out_c[k] = chosen_high + chosen_low
        if k == 0:
            pl.semaphore_wait(barrier, RING - 1)
            for move in moves_e:
                push(*move)
        moves_c.append(
            remote(
                out_c.at[k],
                c_1.at[child_leaf, k],
                c_send.at[0, k],
                c_recv_1.at[child_leaf, k],
                home_1,
            )
        )
        moves_c[k].start()
        chosen = (chosen_high.astype(BF16), chosen_low.astype(BF16))
        for r in range(4):
            cross[r] = cross[r] + dot3(chosen, parts[r], NT)
        gram = gram + dot3(chosen, chosen, NT)

    inv = split(inverse(gram, leaf_rank[device].astype(F32)))
    basis_rows = [dot3(inv, split(cross[r])) for r in range(4)]
    basis_parts = [split(rows) for rows in basis_rows]
    for k in range(STEPS):
        total = jnp.zeros((K, CHUNK), F32)
        for r in range(4):
            rows = pl.ds(r * K, K)
            total = total + dot3(basis_parts[r], (w_high[k, rows, :], w_low[k, rows, :]))
        out_p[k] = total
        moves_p.append(
            remote(
                out_p.at[k],
                p_1.at[child_leaf, k],
                p_send.at[0, k],
                p_recv_1.at[child_leaf, k],
                home_1,
            )
        )
        moves_p[k].start()
    for r in range(4):
        basis_leaf[pl.ds(r * K, K), :] = jnp.transpose(basis_rows[r])
    leaf_out = pltpu.make_async_copy(basis_leaf, leaf_basis, leaf_out_sem)
    leaf_out.start()

    def merge(c_in, p_in, e_in, wait_e, wait_c, wait_p, skeleton_row, rank, rank_a, rank_b, emit_c, emit_p):
        choose = selector(skeleton_row, rank, 2 * K)
        row = lax.broadcasted_iota(jnp.int32, (K, CHUNK), 0)
        mask_a = (row < rank_a).astype(F32)
        mask_b = (row < rank_b).astype(F32)
        wait_e()
        e_top = split(e_in[0])
        e_bottom = split(e_in[1])
        cross_node = jnp.zeros((K, 2 * K), F32)
        gram_node = jnp.zeros((K, K), F32)
        for k in range(STEPS):
            wait_c(k)
            wait_p(k)
            first = split(p_in[0, k])
            second = split(p_in[1, k])
            for child, part in ((0, first), (1, second)):
                kept_high[k, pl.ds(child * K, K), :] = part[0]
                kept_low[k, pl.ds(child * K, K), :] = part[1]
            top = (c_in[0, k] - dot3(e_top, second)) * mask_a
            bottom = (c_in[1, k] - dot3(e_bottom, first)) * mask_b
            stacked = split(jnp.concatenate([top, bottom], axis=0))
            chosen_high = dot(choose, stacked[0])
            chosen_low = dot(choose, stacked[1])
            emit_c(k, chosen_high + chosen_low)
            chosen = (chosen_high.astype(BF16), chosen_low.astype(BF16))
            cross_node = cross_node + dot3(chosen, stacked, NT)
            gram_node = gram_node + dot3(chosen, chosen, NT)
        inv_node = split(inverse(gram_node, rank.astype(F32)))
        basis_node = dot3(inv_node, split(cross_node))
        node_parts = split(basis_node)
        for k in range(STEPS):
            emit_p(k, dot3(node_parts, (kept_high[k], kept_low[k])))
        return jnp.concatenate(
            [jnp.transpose(basis_node[:, :K]), jnp.transpose(basis_node[:, K:])], axis=0
        )

    @pl.when(pos < 4)
    def _():
        id_1 = at_z(node_1)

        def wait_e():
            for child in range(2):
                arrived(e_1.at[child], e_recv_1.at[child])

        def wait_c(k):
            for child in range(2):
                arrived(c_1.at[child, k], c_recv_1.at[child, k])

        def wait_p(k):
            for child in range(2):
                arrived(p_1.at[child, k], p_recv_1.at[child, k])

        def send(buf, sends, recvs, k):
            return remote(buf.at[child_1, k], buf.at[child_1, k], sends.at[1, k], recvs.at[k], home_2)

        def emit_c(k, value):
            c_2[child_1, k] = value

            @pl.when(home_2 != device)
            def _():
                send(c_2, c_send, c_recv_2, k).start()

        def emit_p(k, value):
            p_2[child_1, k] = value

            @pl.when(home_2 != device)
            def _():
                send(p_2, p_send, p_recv_2, k).start()

        basis_buf_1[...] = merge(
            c_1,
            p_1,
            e_1,
            wait_e,
            wait_c,
            wait_p,
            skeleton_1[pl.ds(id_1, 1), :],
            rank_1[id_1],
            leaf_rank[id_1],
            leaf_rank[at_z(node_1 + 4)],
            emit_c,
            emit_p,
        )
        for c in range(2):
            remote(
                basis_buf_1.at[pl.ds(c * K, K)],
                basis_1,
                out_send_1.at[c],
                out_recv.at[0],
                at_z(node_1 + 4 * c),
            ).start()

    is_2 = (pos == 1) | (pos == 2)

    @pl.when(is_2)
    def _():
        id_2 = at_z(node_2)
        other = 1 - child_1

        def wait_e():
            for c in range(2):
                for h in range(2):
                    arrived(e_2.at[c, pl.ds(h * 64, 64)], e_recv_2.at[c, h])

        def wait_c(k):
            arrived(c_2.at[other, k], c_recv_2.at[k])

        def wait_p(k):
            arrived(p_2.at[other, k], p_recv_2.at[k])

        def send(buf, sends, recvs, k):
            return remote(buf.at[child_2, k], buf.at[child_2, k], sends.at[2, k], recvs.at[k], home_3)

        def emit_c(k, value):
            c_3[child_2, k] = value

            @pl.when(home_3 != device)
            def _():
                send(c_3, c_send, c_recv_3, k).start()

        def emit_p(k, value):
            p_3[child_2, k] = value

            @pl.when(home_3 != device)
            def _():
                send(p_3, p_send, p_recv_3, k).start()

        basis_buf_2[...] = merge(
            c_2,
            p_2,
            e_2,
            wait_e,
            wait_c,
            wait_p,
            skeleton_2[pl.ds(id_2, 1), :],
            rank_2[id_2],
            rank_1[id_2],
            rank_1[at_z(node_2 + 2)],
            emit_c,
            emit_p,
        )
        for c in range(2):
            for h in range(2):
                push(
                    basis_buf_2.at[pl.ds(c * K + h * 64, 64)],
                    basis_2,
                    out_send_2.at[c, h],
                    out_recv.at[1],
                    at_z(node_2 + 2 * (2 * h + c)),
                )

    @pl.when(pos == 1)
    def _():
        def wait_e():
            for c in range(2):
                for h in range(4):
                    arrived(e_3.at[c, pl.ds(h * 32, 32)], e_recv_3.at[c, h])

        def wait_c(k):
            arrived(c_3.at[0, k], c_recv_3.at[k])

        def wait_p(k):
            arrived(p_3.at[0, k], p_recv_3.at[k])

        def emit_c(k, value):
            c_top[:, pl.ds(k * CHUNK, CHUNK)] = value
            if k == STEPS - 1:
                for j in range(RING):
                    push(
                        c_top.at[pl.ds(j * 16, 16)],
                        top_samples,
                        top_send_c.at[j],
                        out_recv.at[3],
                        at_z(j),
                    )

        def emit_p(k, value):
            p_top[:, pl.ds(k * CHUNK, CHUNK)] = value
            if k == STEPS - 1:
                for j in range(RING):
                    push(
                        p_top.at[pl.ds(j * 16, 16)],
                        top_projected,
                        top_send_p.at[j],
                        out_recv.at[4],
                        at_z(j),
                    )

        basis_buf_3[...] = merge(
            c_3,
            p_3,
            e_3,
            wait_e,
            wait_c,
            wait_p,
            skeleton_3[pl.ds(rest, 1), :],
            rank_3[rest],
            rank_2[rest],
            rank_2[at_z(1)],
            emit_c,
            emit_p,
        )
        for c in range(2):
            for h in range(4):
                push(
                    basis_buf_3.at[pl.ds(c * K + h * 32, 32)],
                    basis_3,
                    out_send_3.at[c, h],
                    out_recv.at[2],
                    at_z(2 * h + c),
                )

    for move in moves_c + moves_p:
        move.wait_send()
    for move in moves_e:
        pushed(*move)
    leaf_out.wait()

    @pl.when(pos < 4)
    def _():
        @pl.when(home_2 != device)
        def _():
            for k in range(STEPS):
                for buf, sends, recvs in ((c_2, c_send, c_recv_2), (p_2, p_send, p_recv_2)):
                    remote(
                        buf.at[child_1, k], buf.at[child_1, k], sends.at[1, k], recvs.at[k], home_2
                    ).wait_send()

        for c in range(2):
            remote(
                basis_buf_1.at[pl.ds(c * K, K)],
                basis_1,
                out_send_1.at[c],
                out_recv.at[0],
                at_z(node_1 + 4 * c),
            ).wait_send()

    @pl.when(is_2)
    def _():
        @pl.when(home_3 != device)
        def _():
            for k in range(STEPS):
                for buf, sends, recvs in ((c_3, c_send, c_recv_3), (p_3, p_send, p_recv_3)):
                    remote(
                        buf.at[child_2, k], buf.at[child_2, k], sends.at[2, k], recvs.at[k], home_3
                    ).wait_send()

        for c in range(2):
            for h in range(2):
                pushed(
                    basis_buf_2.at[pl.ds(c * K + h * 64, 64)],
                    basis_2,
                    out_send_2.at[c, h],
                    out_recv.at[1],
                    at_z(node_2 + 2 * (2 * h + c)),
                )

    @pl.when(pos == 1)
    def _():
        for j in range(RING):
            pushed(
                c_top.at[pl.ds(j * 16, 16)], top_samples, top_send_c.at[j], out_recv.at[3], at_z(j)
            )
            pushed(
                p_top.at[pl.ds(j * 16, 16)], top_projected, top_send_p.at[j], out_recv.at[4], at_z(j)
            )
        for c in range(2):
            for h in range(4):
                pushed(
                    basis_buf_3.at[pl.ds(c * K + h * 32, 32)],
                    basis_3,
                    out_send_3.at[c, h],
                    out_recv.at[2],
                    at_z(2 * h + c),
                )

    arrived(basis_1, out_recv.at[0])
    arrived(basis_2, out_recv.at[1])
    arrived(basis_3, out_recv.at[2])
    arrived(top_samples, out_recv.at[3])
    arrived(top_projected, out_recv.at[4])


def shards(
    samples,
    test_vectors,
    diag_blocks,
    leaf_skeleton,
    leaf_rank,
    coupling_1,
    coupling_2,
    coupling_3,
    skeleton_1,
    rank_1,
    skeleton_2,
    rank_2,
    skeleton_3,
    rank_3,
):
    stride = lax.axis_size("leaf") // RING
    hbm = pl.BlockSpec(memory_space=pltpu.MemorySpace.HBM)
    vmem = pl.BlockSpec(memory_space=pltpu.MemorySpace.VMEM)
    smem = pl.BlockSpec(memory_space=pltpu.MemorySpace.SMEM)
    dma = pltpu.SemaphoreType.DMA
    slots = pltpu.VMEM((2, STEPS, K, CHUNK), F32)
    blocks = pltpu.VMEM((STEPS, K, CHUNK), F32)

    def kernel(*refs):
        body(stride, *refs)

    return pl.pallas_call(
        kernel,
        name="hss_tree",
        out_shape=(
            jax.ShapeDtypeStruct((LEAF, K), F32),
            jax.ShapeDtypeStruct((K, K), F32),
            jax.ShapeDtypeStruct((K // 2, K), F32),
            jax.ShapeDtypeStruct((K // 4, K), F32),
            jax.ShapeDtypeStruct((K // 8, SAMPLES), F32),
            jax.ShapeDtypeStruct((K // 8, SAMPLES), F32),
        ),
        in_specs=[hbm] * 3 + [vmem] * 7 + [smem] * 4,
        out_specs=(hbm,) * 6,
        scratch_shapes=[
            pltpu.VMEM((STEPS, LEAF, CHUNK), F32),
            pltpu.VMEM((STEPS, LEAF, CHUNK), F32),
            pltpu.VMEM((LEAF, LEAF), F32),
            pltpu.VMEM((LEAF, LEAF), BF16),
            pltpu.VMEM((LEAF, LEAF), BF16),
            pltpu.VMEM((STEPS, LEAF, CHUNK), BF16),
            pltpu.VMEM((STEPS, LEAF, CHUNK), BF16),
            blocks,
            blocks,
            slots,
            slots,
            slots,
            slots,
            slots,
            slots,
            pltpu.VMEM((K, SAMPLES), F32),
            pltpu.VMEM((K, SAMPLES), F32),
            pltpu.VMEM((2, K, K), F32),
            pltpu.VMEM((2, K, K), F32),
            pltpu.VMEM((2, K, K), F32),
            pltpu.VMEM((STEPS, 2 * K, CHUNK), BF16),
            pltpu.VMEM((STEPS, 2 * K, CHUNK), BF16),
            pltpu.VMEM((LEAF, K), F32),
            pltpu.VMEM((2 * K, K), F32),
            pltpu.VMEM((2 * K, K), F32),
            pltpu.VMEM((2 * K, K), F32),
            dma((1 + 2 * STEPS,)),
            dma(()),
            dma((3,)),
            dma((2,)),
            dma((2, 2)),
            dma((2, 4)),
            dma((3, STEPS)),
            dma((3, STEPS)),
            dma((2, STEPS)),
            dma((2, STEPS)),
            dma((STEPS,)),
            dma((STEPS,)),
            dma((STEPS,)),
            dma((STEPS,)),
            dma((2,)),
            dma((2, 2)),
            dma((2, 4)),
            dma((RING,)),
            dma((RING,)),
            dma((5,)),
        ],
        compiler_params=pltpu.CompilerParams(
            collective_id=0, has_side_effects=True, vmem_limit_bytes=48 * 1024 * 1024
        ),
    )(
        samples,
        test_vectors,
        diag_blocks,
        leaf_skeleton,
        skeleton_1,
        skeleton_2,
        skeleton_3,
        coupling_1,
        coupling_2,
        coupling_3,
        leaf_rank,
        rank_1,
        rank_2,
        rank_3,
    )


def solution(mesh):
    rows = P("leaf", None)
    return jax.shard_map(
        shards,
        mesh=mesh,
        in_specs=(rows,) * 4 + (P(),) + (rows,) * 3 + (P(),) * 6,
        out_specs=(rows,) * 6,
        check_vma=False,
    )
```

profile of v0, /device:TPU:12, one launch (start us, length us, event | category | flops | bytes accessed | tf_op | source)
XLA Modules:
  0.0 87.4 jit_solution(10929452619020147207)
XLA Ops:
  0.6 0.0 copy-start
  0.6 1.6 %copy-done = f32[512,1024]{1,0:T(8,128)S(1)} copy-done((f32[512,1024]{1,0:T(8,128)S(1)}, f32[512,1024]{1,0:T(8,128)}, u32[]{:S(2)}) %copy-start) | copy-done | bytes 2097176
  2.2 0.0 copy-start.1
  2.2 1.6 %copy-done.1 = f32[512,1024]{1,0:T(8,128)S(1)} copy-done((f32[512,1024]{1,0:T(8,128)S(1)}, f32[512,1024]{1,0:T(8,128)}, u32[]{:S(2)}) %copy-start.1) | copy-done | bytes 2097176
  3.8 0.0 copy-start.2
  3.8 1.2 %copy-done.2 = f32[512,512]{1,0:T(8,128)S(1)} copy-done((f32[512,512]{1,0:T(8,128)S(1)}, f32[512,512]{1,0:T(8,128)}, u32[]{:S(2)}) %copy-start.2) | copy-done | bytes 1048600
  5.0 0.0 copy-start.3
  5.0 0.8 copy-done.3
  5.9 0.0 copy-start.4
  5.9 0.8 copy-done.4
  6.7 0.0 copy-start.5
  6.7 0.8 copy-done.5
  7.5 0.0 copy-start.6
  7.5 0.8 copy-done.6
  8.2 0.0 copy-start.7
  8.2 0.7 copy-done.7
  9.0 0.0 copy-start.8
  9.0 0.7 copy-done.8
  9.7 0.0 copy-start.9
  9.7 0.7 copy-done.9
  10.4 0.0 copy-start.10
  10.4 0.7 copy-done.10
  11.0 0.0 copy-start.11
  11.0 0.7 copy-done.11
  11.7 0.0 copy-start.12
  11.7 0.7 copy-done.12
  12.3 0.0 copy-start.13
  12.3 0.7 copy-done.13
  13.0 70.6 %hss_tree.1 = (f32[512,128]{1,0:T(8,128)S(1)}, f32[128,128]{1,0:T(8,128)S(1)}, f32[64,128]{1,0:T(8,128)S(1)}, f32[32,128]{1,0:T(8,128)S(1)}, f32[16,1024]{1,0:T(8,128)S(1)}, /*index=5*/f32[16,1024]{1,0:T(8,128)S(1)}) custom-call(f32[512,1024]{1,0:T(8,128)S(1)} %copy-done, f32[512,1024]{1,0:T(8,128)S(1)} %copy-done.1, f32[512,512]{1,0:T(8,128)S(1)} %copy-done.2, ...), custom_call_target="tpu_custom_call" | custom-call | tf_op jit(solution)/shard_map/hss_tree/pallas_call | solution.py:621
  83.6 0.7 copy.26
  84.3 0.6 copy.27
  84.9 0.6 copy.28
  85.5 0.6 copy.29
  86.1 0.6 copy.30
  86.8 0.6 copy.31
Async XLA Ops:
  0.6 1.6 %copy-start = (f32[512,1024]{1,0:T(8,128)S(1)}, f32[512,1024]{1,0:T(8,128)}, u32[]{:S(2)}) copy-start(f32[512,1024]{1,0:T(8,128)} %refs_0_.1) | copy-start | bytes 6291460
  2.2 1.6 %copy-start.1 = (f32[512,1024]{1,0:T(8,128)S(1)}, f32[512,1024]{1,0:T(8,128)}, u32[]{:S(2)}) copy-start(f32[512,1024]{1,0:T(8,128)} %refs_1_.1) | copy-start | bytes 6291460
  3.8 1.2 %copy-start.2 = (f32[512,512]{1,0:T(8,128)S(1)}, f32[512,512]{1,0:T(8,128)}, u32[]{:S(2)}) copy-start(f32[512,512]{1,0:T(8,128)} %refs_2_.1) | copy-start | bytes 3145732
  5.0 0.8 copy-start.3
  5.9 0.8 copy-start.4
  6.7 0.8 copy-start.5
  7.5 0.8 copy-start.6
  8.2 0.7 copy-start.7
  9.0 0.7 copy-start.8
  9.7 0.7 copy-start.9
  10.4 0.7 copy-start.10
  11.0 0.7 copy-start.11
  11.7 0.7 copy-start.12
  12.3 0.7 copy-start.13
where the time goes:
time: 88 us; the launch traced here: 87.4 us
  Pallas kernels  70.6 us (80%)
  local copies, waits for them, and re-layouts  16.1 us (18%)
    pallas_call x1, Pallas kernels, shards(): pl.pallas_call(kernel, name='hss_tree', out_shape=(jax.ShapeDtypeStruct((...  70.6 us
    unnamed x34, local copies, waits for them, and re-layouts  16.1 us

commit v1 on v0

--- a/solution.py
+++ b/solution.py
@@ -77,6 +77,41 @@
     return jnp.concatenate(blocks, axis=1)
 
 
+def products(stack, rows, chosen_high, chosen_low):
+    stack[2 * rows : 2 * rows + K, :] = chosen_high.astype(BF16)
+    stack[2 * rows + K :, :] = chosen_low.astype(BF16)
+    both = dot(stack[...], stack[2 * rows :, :], NT)
+    cross = both[:rows, :K] + (both[:rows, K:] + both[rows : 2 * rows, :K])
+    low_left = both[2 * rows + K :, :K]
+    gram = both[2 * rows : 2 * rows + K, :K] + (both[2 * rows : 2 * rows + K, K:] + low_left)
+    return cross, gram
+
+
+def times(left, right):
+    rows = left[0].shape[0]
+    both = dot(jnp.concatenate(left, axis=0), jnp.concatenate(split(right), axis=1))
+    return both[:rows, :K] + (both[:rows, K:] + both[rows:, :K])
+
+
+def finish(*refs):
+    count = len(refs) // 3
+    sources, results, spare = refs[:count], refs[count : 2 * count], refs[2 * count : 3 * count]
+    sems = refs[3 * count]
+    loads = [
+        pltpu.make_async_copy(sources[i], spare[i], sems.at[0, i]) for i in range(count)
+    ]
+    stores = [
+        pltpu.make_async_copy(spare[i], results[i], sems.at[1, i]) for i in range(count)
+    ]
+    for load in loads:
+        load.start()
+    for load, store in zip(loads, stores):
+        load.wait()
+        store.start()
+    for store in stores:
+        store.wait()
+
+
 def body(
     stride,
     samples,
@@ -102,8 +137,7 @@
     s_buf,
     w_buf,
     d_buf,
-    d_high,
-    d_low,
+    d_parts,
     w_high,
     w_low,
     out_c,
@@ -121,6 +155,9 @@
     e_3,
     kept_high,
     kept_low,
+    stack_leaf,
+    stack_node,
+    cross_leaf,
     basis_leaf,
     basis_buf_1,
     basis_buf_2,
@@ -216,11 +253,9 @@
 
     select = selector(leaf_skeleton[...], leaf_rank[device], LEAF)
     load_d.wait()
-    for r in range(4):
-        rows = pl.ds(r * K, K)
-        high, low = split(d_buf[rows, :])
-        d_high[rows, :] = high
-        d_low[rows, :] = low
+    high, low = split(d_buf[...])
+    d_parts[:LEAF, :] = high
+    d_parts[LEAF:, :] = low
 
     home_e2 = at_pos(2 - z % 2)
     c2, h2 = (z // 2) % 2, z // 4
@@ -243,7 +278,6 @@
         ),
     )
 
-    cross = [jnp.zeros((K, K), F32) for _ in range(4)]
     gram = jnp.zeros((K, K), F32)
     moves_c, moves_p = [], []
     for k in range(STEPS):
@@ -252,18 +286,13 @@
         high, low = split(w_buf[k])
         w_high[k] = high
         w_low[k] = low
-        w_parts = (w_high[k], w_low[k])
-        parts = []
-        chosen_high = jnp.zeros((K, CHUNK), F32)
-        chosen_low = jnp.zeros((K, CHUNK), F32)
-        for r in range(4):
-            rows = pl.ds(r * K, K)
-            local = s_buf[k, rows, :] - dot3((d_high[rows, :], d_low[rows, :]), w_parts)
-            part = split(local)
-            parts.append(part)
-            columns = select[:, r * K : (r + 1) * K]
-            chosen_high = chosen_high + dot(columns, part[0])
-            chosen_low = chosen_low + dot(columns, part[1])
+        both = dot(d_parts[...], w_high[k])
+        local = s_buf[k] - (both[:LEAF] + (both[LEAF:] + dot(d_parts[:LEAF, :], w_low[k])))
+        high, low = split(local)
+        stack_leaf[:LEAF, :] = high
+        stack_leaf[LEAF : 2 * LEAF, :] = low
+        chosen_high = dot(select, stack_leaf[:LEAF, :])
+        chosen_low = dot(select, stack_leaf[LEAF : 2 * LEAF, :])
         out_c[k] = chosen_high + chosen_low
         if k == 0:
             pl.semaphore_wait(barrier, RING - 1)
@@ -279,20 +308,18 @@
             )
         )
         moves_c[k].start()
-        chosen = (chosen_high.astype(BF16), chosen_low.astype(BF16))
-        for r in range(4):
-            cross[r] = cross[r] + dot3(chosen, parts[r], NT)
-        gram = gram + dot3(chosen, chosen, NT)
-
-    inv = split(inverse(gram, leaf_rank[device].astype(F32)))
-    basis_rows = [dot3(inv, split(cross[r])) for r in range(4)]
-    basis_parts = [split(rows) for rows in basis_rows]
+        term, gram_term = products(stack_leaf, LEAF, chosen_high, chosen_low)
+        gram = gram + gram_term
+        if k == 0:
+            cross_leaf[...] = term
+        else:
+            cross_leaf[...] += term
+
+    basis = times(split(cross_leaf[...]), inverse(gram, leaf_rank[device].astype(F32)))
+    turned = jnp.concatenate(split(jnp.transpose(basis)), axis=0)
     for k in range(STEPS):
-        total = jnp.zeros((K, CHUNK), F32)
-        for r in range(4):
-            rows = pl.ds(r * K, K)
-            total = total + dot3(basis_parts[r], (w_high[k, rows, :], w_low[k, rows, :]))
-        out_p[k] = total
+        both = dot(turned, w_high[k])
+        out_p[k] = both[:K] + (both[K:] + dot(turned[:K], w_low[k]))
         moves_p.append(
             remote(
                 out_p.at[k],
@@ -303,46 +330,56 @@
             )
         )
         moves_p[k].start()
-    for r in range(4):
-        basis_leaf[pl.ds(r * K, K), :] = jnp.transpose(basis_rows[r])
+    basis_leaf[...] = basis
     leaf_out = pltpu.make_async_copy(basis_leaf, leaf_basis, leaf_out_sem)
     leaf_out.start()
 
     def merge(c_in, p_in, e_in, wait_e, wait_c, wait_p, skeleton_row, rank, rank_a, rank_b, emit_c, emit_p):
         choose = selector(skeleton_row, rank, 2 * K)
-        row = lax.broadcasted_iota(jnp.int32, (K, CHUNK), 0)
-        mask_a = (row < rank_a).astype(F32)
-        mask_b = (row < rank_b).astype(F32)
+        row = lax.broadcasted_iota(jnp.int32, (2 * K, CHUNK), 0)
+        live = row < jnp.where(row < K, rank_a, K + rank_b)
         wait_e()
-        e_top = split(e_in[0])
-        e_bottom = split(e_in[1])
-        cross_node = jnp.zeros((K, 2 * K), F32)
+        zero = jnp.zeros((K, K), BF16)
+        top = split(e_in[0])
+        bottom = split(e_in[1])
+        cross_parts = [
+            jnp.concatenate(
+                [
+                    jnp.concatenate([zero, top[part]], axis=1),
+                    jnp.concatenate([bottom[part], zero], axis=1),
+                ],
+                axis=0,
+            )
+            for part in range(2)
+        ]
+        couple = jnp.concatenate(cross_parts, axis=0)
+        cross = jnp.zeros((2 * K, K), F32)
         gram_node = jnp.zeros((K, K), F32)
         for k in range(STEPS):
             wait_c(k)
             wait_p(k)
-            first = split(p_in[0, k])
-            second = split(p_in[1, k])
-            for child, part in ((0, first), (1, second)):
+            for child in range(2):
+                part = split(p_in[child, k])
                 kept_high[k, pl.ds(child * K, K), :] = part[0]
                 kept_low[k, pl.ds(child * K, K), :] = part[1]
-            top = (c_in[0, k] - dot3(e_top, second)) * mask_a
-            bottom = (c_in[1, k] - dot3(e_bottom, first)) * mask_b
-            stacked = split(jnp.concatenate([top, bottom], axis=0))
-            chosen_high = dot(choose, stacked[0])
-            chosen_low = dot(choose, stacked[1])
+            both = dot(couple, kept_high[k])
+            change = both[: 2 * K] + (both[2 * K :] + dot(cross_parts[0], kept_low[k]))
+            stacked = jnp.concatenate([c_in[0, k], c_in[1, k]], axis=0) - change
+            high, low = split(jnp.where(live, stacked, 0.0))
+            stack_node[: 2 * K, :] = high
+            stack_node[2 * K : 4 * K, :] = low
+            chosen_high = dot(choose, high)
+            chosen_low = dot(choose, low)
             emit_c(k, chosen_high + chosen_low)
-            chosen = (chosen_high.astype(BF16), chosen_low.astype(BF16))
-            cross_node = cross_node + dot3(chosen, stacked, NT)
-            gram_node = gram_node + dot3(chosen, chosen, NT)
-        inv_node = split(inverse(gram_node, rank.astype(F32)))
-        basis_node = dot3(inv_node, split(cross_node))
-        node_parts = split(basis_node)
+            term, gram_term = products(stack_node, 2 * K, chosen_high, chosen_low)
+            cross = cross + term
+            gram_node = gram_node + gram_term
+        basis = times(split(cross), inverse(gram_node, rank.astype(F32)))
+        turned = jnp.concatenate(split(jnp.transpose(basis)), axis=0)
         for k in range(STEPS):
-            emit_p(k, dot3(node_parts, (kept_high[k], kept_low[k])))
-        return jnp.concatenate(
-            [jnp.transpose(basis_node[:, :K]), jnp.transpose(basis_node[:, K:])], axis=0
-        )
+            both = dot(turned, kept_high[k])
+            emit_p(k, both[:K] + (both[K:] + dot(turned[:K], kept_low[k])))
+        return basis
 
     @pl.when(pos < 4)
     def _():
@@ -618,25 +655,19 @@
     def kernel(*refs):
         body(stride, *refs)
 
-    return pl.pallas_call(
+    shapes = ((LEAF, K), (K, K), (K // 2, K), (K // 4, K), (K // 8, SAMPLES), (K // 8, SAMPLES))
+    results = tuple(jax.ShapeDtypeStruct(shape, F32) for shape in shapes)
+    values = pl.pallas_call(
         kernel,
         name="hss_tree",
-        out_shape=(
-            jax.ShapeDtypeStruct((LEAF, K), F32),
-            jax.ShapeDtypeStruct((K, K), F32),
-            jax.ShapeDtypeStruct((K // 2, K), F32),
-            jax.ShapeDtypeStruct((K // 4, K), F32),
-            jax.ShapeDtypeStruct((K // 8, SAMPLES), F32),
-            jax.ShapeDtypeStruct((K // 8, SAMPLES), F32),
-        ),
+        out_shape=results,
         in_specs=[hbm] * 3 + [vmem] * 7 + [smem] * 4,
         out_specs=(hbm,) * 6,
         scratch_shapes=[
             pltpu.VMEM((STEPS, LEAF, CHUNK), F32),
             pltpu.VMEM((STEPS, LEAF, CHUNK), F32),
             pltpu.VMEM((LEAF, LEAF), F32),
-            pltpu.VMEM((LEAF, LEAF), BF16),
-            pltpu.VMEM((LEAF, LEAF), BF16),
+            pltpu.VMEM((2 * LEAF, LEAF), BF16),
             pltpu.VMEM((STEPS, LEAF, CHUNK), BF16),
             pltpu.VMEM((STEPS, LEAF, CHUNK), BF16),
             blocks,
@@ -654,6 +685,9 @@
             pltpu.VMEM((2, K, K), F32),
             pltpu.VMEM((STEPS, 2 * K, CHUNK), BF16),
             pltpu.VMEM((STEPS, 2 * K, CHUNK), BF16),
+            pltpu.VMEM((2 * LEAF + 2 * K, CHUNK), BF16),
+            pltpu.VMEM((6 * K, CHUNK), BF16),
+            pltpu.VMEM((LEAF, K), F32),
             pltpu.VMEM((LEAF, K), F32),
             pltpu.VMEM((2 * K, K), F32),
             pltpu.VMEM((2 * K, K), F32),
@@ -680,7 +714,7 @@
             dma((5,)),
         ],
         compiler_params=pltpu.CompilerParams(
-            collective_id=0, has_side_effects=True, vmem_limit_bytes=48 * 1024 * 1024
+            collective_id=0, has_side_effects=True, vmem_limit_bytes=67043328
         ),
     )(
         samples,
@@ -698,6 +732,15 @@
         rank_2,
         rank_3,
     )
+    return pl.pallas_call(
+        finish,
+        name="hss_finish",
+        out_shape=results,
+        in_specs=[hbm] * 6,
+        out_specs=(hbm,) * 6,
+        scratch_shapes=[pltpu.VMEM(shape, F32) for shape in shapes] + [dma((2, 6))],
+        compiler_params=pltpu.CompilerParams(vmem_limit_bytes=67043328),
+    )(*values)
 
 
 def solution(mesh):

time: 88 us -> 72.6 us (0.82)
  local copies, waits for them, and re-layouts: 16.1 us -> 0 us
  Pallas kernels: 70.6 us -> 71.6 us
    unnamed x34 -> x0, local copies, waits for them, and re-layouts: 16.1 us -> none
    pallas_call x1 -> x2, Pallas kernels: 70.6 us -> 71.6 us  [the longest x1 69.8 us: shards(): pl.pallas_call(kernel, name='hss_tree', out_shape=results, in_specs=[hbm]...]
where the time goes in v1:
time: 72.6 us; the launch traced here: 72.4 us
  Pallas kernels  71.6 us (99%)
  between operations  0.81 us (1%)
    pallas_call x1, Pallas kernels, shards(): pl.pallas_call(kernel, name='hss_tree', out_shape=results, in_specs=[hbm]...  69.8 us
    pallas_call x1, Pallas kernels, shards(): pl.pallas_call(finish, name='hss_finish', out_shape=results, in_specs=[hb...  1.83 us

profile of v1, /device:TPU:12, one launch (start us, length us, event | category | flops | bytes accessed | tf_op | source)
XLA Modules:
  0.0 72.4 jit_solution(4124951924665061580)
XLA Ops:
  0.6 69.8 %hss_tree.1 = (f32[512,128]{1,0:T(8,128)}, f32[128,128]{1,0:T(8,128)}, f32[64,128]{1,0:T(8,128)}, f32[32,128]{1,0:T(8,128)}, f32[16,1024]{1,0:T(8,128)}, /*index=5*/f32[16,1024]{1,0:T(8,128)}) custom-call(f32[512,1024]{1,0:T(8,128)} %refs_0_.1, f32[512,1024]{1,0:T(8,128)} %refs_1_.1, f32[512,512]{1,0:T(8,128)} %refs_2_.1, s32[1,128]{1,0:T(1,128)} %refs_3_.1, ...), custom_call_target="tpu_custom_call" | custom-call | tf_op jit(solution)/shard_map/hss_tree/pallas_call | solution.py:660
  70.4 1.8 %hss_finish.1 = (f32[512,128]{1,0:T(8,128)}, f32[128,128]{1,0:T(8,128)}, f32[64,128]{1,0:T(8,128)}, f32[32,128]{1,0:T(8,128)}, f32[16,1024]{1,0:T(8,128)}, /*index=5*/f32[16,1024]{1,0:T(8,128)}) custom-call(f32[512,128]{1,0:T(8,128)} %get-tuple-element.12.refs_0_, f32[128,128]{1,0:T(8,128)} %get-tuple-element.13.refs_1_, ...), custom_call_target="tpu_custom_call" | custom-call | tf_op jit(solution)/shard_map/hss_finish/pallas_call | solution.py:735
